TPU v7x, 128 devices: a whole 4x4x4 slice. The times are simulated.
128 devices in a mesh: walk: 16 (over y_hi, z, core), band: 8 (over y_lo, x).
Axes of the slice: x: 4, y: 4 (y_hi: 2, y_lo: 2; y = y_hi * 2 + y_lo), z: 4, core: 2. Of those that a mesh axis runs over, the one named last changes fastest.
Arguments:
- positions: float32 [2, 49152], P(None, 'walk'), may hold values from 0 to 1
- coefficients: bfloat16 [2, 18432, 1024], P(None, 'walk', 'band')
- lattice: int32 [2, 18432], replicated, may hold values from -76 to 76
- spin_labels: int32 [49152], P('walk'), may hold values from 0 to 1
- occupied: int32 [2, 48], replicated, may hold values from 0 to 1023
- features: bfloat16 [49152, 256], P('walk'), may hold values from -6 to 6
- orbital_head: bfloat16 [256, 192], replicated, may hold values from -0.029907227 to 0.029907227
Outputs:
- gradient: float32 [256, 192], replicated
All inputs are finite; a program needn't handle non-finite values.
Results may differ from a plain program's by a relative error of at most 0.0003.
Values may be sent and summed in bfloat16 or wider, within the bound.
No kernel may reach another device: no remote copies, remote signals or barrier semaphores. Data moves between devices by JAX's collectives and lax.ppermute only.
A program may use at most 128 MiB of HBM per device.

v0:
```python
import jax
import jax.numpy as jnp
from jax import lax
from jax.sharding import PartitionSpec as P

E = 96
TWO_PI = 6.283185307179586


def orbital_block(pos_x, pos_y, lat_x, lat_y, right_cos, right_sin):
    phase_angle = TWO_PI * (pos_x[:, None] * lat_x[None, :] + pos_y[:, None] * lat_y[None, :])
    cosine = jnp.cos(phase_angle)
    sine_part = jnp.sin(phase_angle)
    first = jnp.dot(
        cosine, right_cos, precision=lax.Precision.HIGHEST, preferred_element_type=jnp.float32
    )
    second = jnp.dot(
        sine_part, right_sin, precision=lax.Precision.HIGHEST, preferred_element_type=jnp.float32
    )
    return first + second


def spin_columns(orbitals, spin_labels):
    orbital_count = orbitals.shape[1] // 4
    spin_up = (spin_labels == 0)[:, None]
    real_pick = jnp.where(
        spin_up, orbitals[:, :orbital_count], orbitals[:, orbital_count : 2 * orbital_count]
    )
    imag_pick = jnp.where(
        spin_up,
        orbitals[:, 2 * orbital_count : 3 * orbital_count],
        orbitals[:, 3 * orbital_count :],
    )
    return jnp.concatenate([real_pick, imag_pick], axis=1)


def fit_from_target(target, spin_labels, features, orbital_head, walkers):
    half_width = target.shape[1]
    spin_up = (spin_labels == 0)[:, None]
    net_all = jnp.dot(features, orbital_head, preferred_element_type=jnp.float32)
    net_value = jnp.where(spin_up, net_all[:, :half_width], net_all[:, half_width:])
    scaled = (net_value - target) / walkers
    blank_rows = jnp.zeros_like(scaled)
    spread_rows = jnp.concatenate(
        [jnp.where(spin_up, scaled, blank_rows), jnp.where(spin_up, blank_rows, scaled)], axis=1
    )
    return lax.dot_general(
        features.astype(jnp.float32),
        spread_rows,
        (((0,), (0,)), ((), ())),
        precision=lax.Precision.HIGHEST,
        preferred_element_type=jnp.float32,
    )


def fit_gradient(orbitals, spin_labels, features, orbital_head, walkers):
    target = spin_columns(orbitals, spin_labels)
    return fit_from_target(target, spin_labels, features, orbital_head, walkers)


def local(positions, coefficients, lattice, spin_labels, occupied, features, orbital_head):
    walk_count = lax.axis_size("walk")
    band_count = lax.axis_size("band")
    band_index = lax.axis_index("band")
    occ_flat = occupied.reshape(-1)
    wave_count = lattice.shape[1]
    gathered = lax.all_gather(coefficients, "walk", axis=1, tiled=True)
    band_panel = lax.all_to_all(gathered, "band", split_axis=1, concat_axis=2, tiled=True)
    picked = jnp.take(band_panel, occ_flat, axis=2)
    local_lattice = lax.dynamic_slice_in_dim(
        lattice, band_index * (wave_count // band_count), wave_count // band_count, 1
    )
    right_cos = jnp.concatenate([picked[0], picked[1]], axis=1).astype(jnp.float32)
    right_sin = jnp.concatenate([-picked[1], picked[0]], axis=1).astype(jnp.float32)
    lat_x = local_lattice[0].astype(jnp.float32)
    lat_y = local_lattice[1].astype(jnp.float32)
    local_count = positions.shape[1]
    block_rows = min(384, local_count)
    block_count = local_count // block_rows
    pos_x = positions[0].reshape(block_count, block_rows)
    pos_y = positions[1].reshape(block_count, block_rows)
    partial_value = lax.map(
        lambda coords: orbital_block(coords[0], coords[1], lat_x, lat_y, right_cos, right_sin),
        (pos_x, pos_y),
    )
    partial_value = partial_value.reshape(local_count, right_cos.shape[1])
    walkers = float(walk_count * local_count // E)
    orbitals = lax.psum(partial_value, "band")
    gradient = fit_gradient(orbitals, spin_labels, features, orbital_head, walkers)
    return lax.psum(gradient, "walk")


def solution(mesh):
    return jax.shard_map(
        local,
        mesh=mesh,
        in_specs=(
            P(None, "walk"),
            P(None, "walk", "band"),
            P(),
            P("walk"),
            P(),
            P("walk", None),
            P(),
        ),
        out_specs=P(),
        check_vma=False,
    )
```

profile of v0, /device:TPU:0, one launch (start us, length us, event | category | flops | bytes accessed | tf_op | source)
XLA Modules:
  0.0 891.4 jit_solution(2126646476932792642)
XLA Ops:
  6.5 6.1 copy.31
  12.7 79.9 %all-gather.2.cloned.1.call-done = bf16[2,18432,128]{2,0,1:T(2,128)(2,1)} async-done(((bf16[2,1152,128]{2,0,1:T(2,128)(2,1)}), bf16[2,18432,128]{2,0,1:T(2,128)(2,1)}) %all-gather.2.cloned.1.call-update) | async-done | bytes 9437200 | tf_op jit(solution)/shard_map/all_gather | solution.py:67
  92.5 5.0 all-to-all-start
  97.7 0.1 reshape.52
  97.7 0.1 reshape.51
  97.8 0.1 slice_reduce_fusion
  97.9 0.9 fusion.32
  98.9 105.0 %all-to-all-done = bf16[2,18432,128]{2,0,1:T(2,128)(2,1)} async-done(((bf16[2,18432,128]{2,0,1:T(2,128)(2,1)}), bf16[2,18432,128]{2,0,1:T(2,128)(2,1)}, u32[]{:S(2)}, u32[]{:S(2)}) %all-to-all-start) | async-done | bytes 9437216 | tf_op jit(solution)/shard_map/all_to_all | solution.py:68
  203.9 10.1 %copy.32 = bf16[2,18432,128]{2,1,0:T(8,128)(2,1)} copy(bf16[2,18432,128]{2,0,1:T(2,128)(2,1)} %all-to-all-done) | data formatting | bytes 18874368 | tf_op jit(solution)/shard_map/all_to_all | solution.py:68
  214.0 12.9 %copy.33 = bf16[2,2304,8,128]{1,3,2,0:T(8,128)(2,1)} copy(bf16[2,2304,8,128]{3,1,2,0:T(8,128)(2,1)} %bitcast.33) | data formatting | bytes 18874368 | tf_op jit(solution)/shard_map/all_to_all | solution.py:68
  226.9 18.4 %copy.34 = bf16[2,2304,1024]{1,0,2:T(2,128)(2,1)} copy(bf16[2,2304,1024]{1,2,0:T(8,128)(2,1)} %bitcast.34) | data formatting | bytes 18874368 | tf_op jit(solution)/shard_map/all_to_all | solution.py:68
  245.3 6.1 gather_fusion
  251.4 0.8 fusion.31
  252.2 1.2 fusion.37
  253.4 0.1 fusion.36
  253.5 0.1 copy.46
  253.6 1.5 maximum_convert_fusion.1
  255.0 3.0 copy.35
  258.0 1.9 copy.36
  259.9 364.3 %while.10 = (s32[]{:T(128)}, f32[8,384,192]{1,0,2:T(8,128)}, f32[8,384]{1,0:T(8,128)S(1)}, f32[2304]{0:T(1024)S(1)}, f32[8,384]{1,0:T(8,128)S(1)}, /*index=5*/f3...) while((s32[]{:T(128)}, f32[8,384,192]{1,0,2:T(8,128)}, ...), condition=%wide.region_1.2_spmd, body=%wide.region_0.1_spmd.sunk | while | flops 4084015104 | bytes 12730505 | solution.py:82
  282.6 18.3 %fusion.54 = f32[384,192]{0,1:T(8,128)S(1)} fusion(f32[2304,192]{1,0:T(8,128)} %get-tuple-element.200, f32[2304]{0:T(1024)S(1)} %get-tuple-element.198, f32[384]{0:T(512)S(1)} %get-tuple-element.171, f32[2304]{0:T(1024)S(1)} %get-tuple-element.196, f32[384]{0:T(512)S(1)} %get-tuple-element.172), kind=kOutput, calls=%fused_computation.1.clone.1 | convolution fusion | flops 2041970688 | bytes 2085888 | tf_op jit(solution)/shard_map/while/body/eval_jaxpr/dot_general | solution.py:17
  300.9 16.4 %fusion.55 = f32[1,384,192]{1,2,0:T(8,128)S(1)} fusion(f32[384,192]{0,1:T(8,128)S(1)} %fusion.54, f32[2304,192]{1,0:T(8,128)S(1)} %copy-done.2, f32[2304]{0:T(1024)S(1)} %get-tuple-element.198, f32[384]{0:T(512)S(1)} %get-tuple-element.171, f32[2304]{0:T(1024)S(1)} %get-tuple-element.196, f32[384]{0:T(512)S(1)} %get-tuple-element.172), kind=kOutput, calls=%fused_computation.17.clone.1 | convolution fusion | flops 2042044416 | bytes 2380800 | tf_op jit(solution)/shard_map/while/body/eval_jaxpr/dot_general | solution.py:14
  317.4 0.3 copy.48
  317.7 7.3 dynamic_update_slice.5
  325.0 18.3 %fusion.54 = f32[384,192]{0,1:T(8,128)S(1)} fusion(f32[2304,192]{1,0:T(8,128)} %get-tuple-element.200, f32[2304]{0:T(1024)S(1)} %get-tuple-element.198, f32[384]{0:T(512)S(1)} %get-tuple-element.171, f32[2304]{0:T(1024)S(1)} %get-tuple-element.196, f32[384]{0:T(512)S(1)} %get-tuple-element.172), kind=kOutput, calls=%fused_computation.1.clone.1 | convolution fusion | flops 2041970688 | bytes 2085888 | tf_op jit(solution)/shard_map/while/body/eval_jaxpr/dot_general | solution.py:17
  343.3 16.4 %fusion.55 = f32[1,384,192]{1,2,0:T(8,128)S(1)} fusion(f32[384,192]{0,1:T(8,128)S(1)} %fusion.54, f32[2304,192]{1,0:T(8,128)S(1)} %copy-done.2, f32[2304]{0:T(1024)S(1)} %get-tuple-element.198, f32[384]{0:T(512)S(1)} %get-tuple-element.171, f32[2304]{0:T(1024)S(1)} %get-tuple-element.196, f32[384]{0:T(512)S(1)} %get-tuple-element.172), kind=kOutput, calls=%fused_computation.17.clone.1 | convolution fusion | flops 2042044416 | bytes 2380800 | tf_op jit(solution)/shard_map/while/body/eval_jaxpr/dot_general | solution.py:14
  359.7 0.3 copy.48
  360.0 7.3 dynamic_update_slice.5
  367.4 18.3 %fusion.54 = f32[384,192]{0,1:T(8,128)S(1)} fusion(f32[2304,192]{1,0:T(8,128)} %get-tuple-element.200, f32[2304]{0:T(1024)S(1)} %get-tuple-element.198, f32[384]{0:T(512)S(1)} %get-tuple-element.171, f32[2304]{0:T(1024)S(1)} %get-tuple-element.196, f32[384]{0:T(512)S(1)} %get-tuple-element.172), kind=kOutput, calls=%fused_computation.1.clone.1 | convolution fusion | flops 2041970688 | bytes 2085888 | tf_op jit(solution)/shard_map/while/body/eval_jaxpr/dot_general | solution.py:17
  385.7 16.4 %fusion.55 = f32[1,384,192]{1,2,0:T(8,128)S(1)} fusion(f32[384,192]{0,1:T(8,128)S(1)} %fusion.54, f32[2304,192]{1,0:T(8,128)S(1)} %copy-done.2, f32[2304]{0:T(1024)S(1)} %get-tuple-element.198, f32[384]{0:T(512)S(1)} %get-tuple-element.171, f32[2304]{0:T(1024)S(1)} %get-tuple-element.196, f32[384]{0:T(512)S(1)} %get-tuple-element.172), kind=kOutput, calls=%fused_computation.17.clone.1 | convolution fusion | flops 2042044416 | bytes 2380800 | tf_op jit(solution)/shard_map/while/body/eval_jaxpr/dot_general | solution.py:14
  402.1 0.3 copy.48
  402.4 7.3 dynamic_update_slice.5
  409.7 18.3 %fusion.54 = f32[384,192]{0,1:T(8,128)S(1)} fusion(f32[2304,192]{1,0:T(8,128)} %get-tuple-element.200, f32[2304]{0:T(1024)S(1)} %get-tuple-element.198, f32[384]{0:T(512)S(1)} %get-tuple-element.171, f32[2304]{0:T(1024)S(1)} %get-tuple-element.196, f32[384]{0:T(512)S(1)} %get-tuple-element.172), kind=kOutput, calls=%fused_computation.1.clone.1 | convolution fusion | flops 2041970688 | bytes 2085888 | tf_op jit(solution)/shard_map/while/body/eval_jaxpr/dot_general | solution.py:17
  428.1 16.4 %fusion.55 = f32[1,384,192]{1,2,0:T(8,128)S(1)} fusion(f32[384,192]{0,1:T(8,128)S(1)} %fusion.54, f32[2304,192]{1,0:T(8,128)S(1)} %copy-done.2, f32[2304]{0:T(1024)S(1)} %get-tuple-element.198, f32[384]{0:T(512)S(1)} %get-tuple-element.171, f32[2304]{0:T(1024)S(1)} %get-tuple-element.196, f32[384]{0:T(512)S(1)} %get-tuple-element.172), kind=kOutput, calls=%fused_computation.17.clone.1 | convolution fusion | flops 2042044416 | bytes 2380800 | tf_op jit(solution)/shard_map/while/body/eval_jaxpr/dot_general | solution.py:14
  444.5 0.3 copy.48
  444.8 7.3 dynamic_update_slice.5
  452.1 18.3 %fusion.54 = f32[384,192]{0,1:T(8,128)S(1)} fusion(f32[2304,192]{1,0:T(8,128)} %get-tuple-element.200, f32[2304]{0:T(1024)S(1)} %get-tuple-element.198, f32[384]{0:T(512)S(1)} %get-tuple-element.171, f32[2304]{0:T(1024)S(1)} %get-tuple-element.196, f32[384]{0:T(512)S(1)} %get-tuple-element.172), kind=kOutput, calls=%fused_computation.1.clone.1 | convolution fusion | flops 2041970688 | bytes 2085888 | tf_op jit(solution)/shard_map/while/body/eval_jaxpr/dot_general | solution.py:17
  470.4 16.4 %fusion.55 = f32[1,384,192]{1,2,0:T(8,128)S(1)} fusion(f32[384,192]{0,1:T(8,128)S(1)} %fusion.54, f32[2304,192]{1,0:T(8,128)S(1)} %copy-done.2, f32[2304]{0:T(1024)S(1)} %get-tuple-element.198, f32[384]{0:T(512)S(1)} %get-tuple-element.171, f32[2304]{0:T(1024)S(1)} %get-tuple-element.196, f32[384]{0:T(512)S(1)} %get-tuple-element.172), kind=kOutput, calls=%fused_computation.17.clone.1 | convolution fusion | flops 2042044416 | bytes 2380800 | tf_op jit(solution)/shard_map/while/body/eval_jaxpr/dot_general | solution.py:14
  486.9 0.3 copy.48
  487.2 7.3 dynamic_update_slice.5
  494.5 18.3 %fusion.54 = f32[384,192]{0,1:T(8,128)S(1)} fusion(f32[2304,192]{1,0:T(8,128)} %get-tuple-element.200, f32[2304]{0:T(1024)S(1)} %get-tuple-element.198, f32[384]{0:T(512)S(1)} %get-tuple-element.171, f32[2304]{0:T(1024)S(1)} %get-tuple-element.196, f32[384]{0:T(512)S(1)} %get-tuple-element.172), kind=kOutput, calls=%fused_computation.1.clone.1 | convolution fusion | flops 2041970688 | bytes 2085888 | tf_op jit(solution)/shard_map/while/body/eval_jaxpr/dot_general | solution.py:17
  512.8 16.4 %fusion.55 = f32[1,384,192]{1,2,0:T(8,128)S(1)} fusion(f32[384,192]{0,1:T(8,128)S(1)} %fusion.54, f32[2304,192]{1,0:T(8,128)S(1)} %copy-done.2, f32[2304]{0:T(1024)S(1)} %get-tuple-element.198, f32[384]{0:T(512)S(1)} %get-tuple-element.171, f32[2304]{0:T(1024)S(1)} %get-tuple-element.196, f32[384]{0:T(512)S(1)} %get-tuple-element.172), kind=kOutput, calls=%fused_computation.17.clone.1 | convolution fusion | flops 2042044416 | bytes 2380800 | tf_op jit(solution)/shard_map/while/body/eval_jaxpr/dot_general | solution.py:14
  529.2 0.3 copy.48
  529.5 7.3 dynamic_update_slice.5
  536.9 18.3 %fusion.54 = f32[384,192]{0,1:T(8,128)S(1)} fusion(f32[2304,192]{1,0:T(8,128)} %get-tuple-element.200, f32[2304]{0:T(1024)S(1)} %get-tuple-element.198, f32[384]{0:T(512)S(1)} %get-tuple-element.171, f32[2304]{0:T(1024)S(1)} %get-tuple-element.196, f32[384]{0:T(512)S(1)} %get-tuple-element.172), kind=kOutput, calls=%fused_computation.1.clone.1 | convolution fusion | flops 2041970688 | bytes 2085888 | tf_op jit(solution)/shard_map/while/body/eval_jaxpr/dot_general | solution.py:17
  555.2 16.4 %fusion.55 = f32[1,384,192]{1,2,0:T(8,128)S(1)} fusion(f32[384,192]{0,1:T(8,128)S(1)} %fusion.54, f32[2304,192]{1,0:T(8,128)S(1)} %copy-done.2, f32[2304]{0:T(1024)S(1)} %get-tuple-element.198, f32[384]{0:T(512)S(1)} %get-tuple-element.171, f32[2304]{0:T(1024)S(1)} %get-tuple-element.196, f32[384]{0:T(512)S(1)} %get-tuple-element.172), kind=kOutput, calls=%fused_computation.17.clone.1 | convolution fusion | flops 2042044416 | bytes 2380800 | tf_op jit(solution)/shard_map/while/body/eval_jaxpr/dot_general | solution.py:14
  571.6 0.3 copy.48
  571.9 7.3 dynamic_update_slice.5
  579.2 18.3 %fusion.54 = f32[384,192]{0,1:T(8,128)S(1)} fusion(f32[2304,192]{1,0:T(8,128)} %get-tuple-element.200, f32[2304]{0:T(1024)S(1)} %get-tuple-element.198, f32[384]{0:T(512)S(1)} %get-tuple-element.171, f32[2304]{0:T(1024)S(1)} %get-tuple-element.196, f32[384]{0:T(512)S(1)} %get-tuple-element.172), kind=kOutput, calls=%fused_computation.1.clone.1 | convolution fusion | flops 2041970688 | bytes 2085888 | tf_op jit(solution)/shard_map/while/body/eval_jaxpr/dot_general | solution.py:17
  597.6 16.4 %fusion.55 = f32[1,384,192]{1,2,0:T(8,128)S(1)} fusion(f32[384,192]{0,1:T(8,128)S(1)} %fusion.54, f32[2304,192]{1,0:T(8,128)S(1)} %copy-done.2, f32[2304]{0:T(1024)S(1)} %get-tuple-element.198, f32[384]{0:T(512)S(1)} %get-tuple-element.171, f32[2304]{0:T(1024)S(1)} %get-tuple-element.196, f32[384]{0:T(512)S(1)} %get-tuple-element.172), kind=kOutput, calls=%fused_computation.17.clone.1 | convolution fusion | flops 2042044416 | bytes 2380800 | tf_op jit(solution)/shard_map/while/body/eval_jaxpr/dot_general | solution.py:14
  614.0 0.3 copy.48
  614.3 7.3 dynamic_update_slice.5
  624.2 3.5 copy.42
  627.8 0.0 all-reduce.5.cloned.1.call-start
  627.8 0.6 copy-done.5
  628.4 0.2 copy-done.3
  628.6 2.1 fusion.38
  630.7 114.0 %all-reduce.3.cloned.1.call-done = f32[3072,192]{0,1:T(8,128)} async-done(((f32[3072,192]{0,1:T(8,128)}), f32[3072,192]{0,1:T(8,128)}) %all-reduce.3.cloned.1.call-update) | async-done | bytes 2359312 | tf_op jit(solution)/shard_map/psum | solution.py:88
  744.7 1.9 slice_select_fusion.2
  746.6 0.5 copy-done.1
  747.1 0.4 broadcast_select_fusion.2
  747.5 1.9 fusion.28
  749.4 133.6 %all-reduce.5.cloned.1.call-done = f32[256,192]{0,1:T(8,128)} async-done(((f32[256,192]{0,1:T(8,128)}), f32[256,192]{0,1:T(8,128)}) %all-reduce.5.cloned.1.call-update) | async-done | bytes 196624 | tf_op jit(solution)/shard_map/psum | solution.py:90
  883.0 1.6 copy.58
  (45 shorter events, 0.4 us)
Async XLA Ops:
  6.5 621.9 %copy-start = (bf16[3072,256]{1,0:T(8,128)(2,1)S(1)}, bf16[3072,256]{1,0:T(8,128)(2,1)}, u32[]{:S(2)}) copy-start(bf16[3072,256]{1,0:T(8,128)(2,1)} %param.14) | copy-start | bytes 4718596
  6.5 86.0 %all-gather.2.cloned.1.call-start = ((), (), s32[]{:S(2)}) async-start(), calls=%async_computation.1 | async-start | bytes 10027008 | tf_op jit(solution)/shard_map/all_gather | solution.py:67
  12.6 85.0 %copy-start.6 = (s32[2,48]{1,0:T(2,128)S(1)}, s32[2,48]{1,0:T(2,128)}, u32[]{:S(2)}) copy-start(s32[2,48]{1,0:T(2,128)} %param.13) | copy-start | bytes 1156
  12.6 85.2 %copy-start.4 = (f32[2,3072]{1,0:T(2,128)S(1)}, f32[2,3072]{1,0:T(2,128)}, u32[]{:S(2)}) copy-start(f32[2,3072]{1,0:T(2,128)} %param.9) | copy-start | bytes 73732
  92.5 111.3 %all-to-all-start = ((bf16[2,18432,128]{2,0,1:T(2,128)(2,1)}), bf16[2,18432,128]{2,0,1:T(2,128)(2,1)}, u32[]{:S(2)}, u32[]{:S(2)}) async-start(bf16[2,18432,128]{2,0,1:T(2,128)(2,1)} %all-gather.2.cloned.1.call-done), calls=%async_computation | async-start | bytes 18874368 | tf_op jit(solution)/shard_map/all_to_all | solution.py:68
  97.6 647.1 %all-reduce.3.cloned.1.call-start = ((), (), s32[]{:S(2)}) async-start(), calls=%async_computation.2 | async-start | bytes 4718592 | tf_op jit(solution)/shard_map/psum | solution.py:88
  282.6 18.3 %copy-start.2 = (f32[2304,192]{1,0:T(8,128)S(1)}, f32[2304,192]{1,0:T(8,128)}, u32[]{:S(2)}) copy-start(f32[2304,192]{1,0:T(8,128)} %get-tuple-element.199) | copy-start | bytes 5308420 | tf_op jit(solution)/shard_map/while
  325.0 18.3 %copy-start.2 = (f32[2304,192]{1,0:T(8,128)S(1)}, f32[2304,192]{1,0:T(8,128)}, u32[]{:S(2)}) copy-start(f32[2304,192]{1,0:T(8,128)} %get-tuple-element.199) | copy-start | bytes 5308420 | tf_op jit(solution)/shard_map/while
  367.3 18.3 %copy-start.2 = (f32[2304,192]{1,0:T(8,128)S(1)}, f32[2304,192]{1,0:T(8,128)}, u32[]{:S(2)}) copy-start(f32[2304,192]{1,0:T(8,128)} %get-tuple-element.199) | copy-start | bytes 5308420 | tf_op jit(solution)/shard_map/while
  409.7 18.3 %copy-start.2 = (f32[2304,192]{1,0:T(8,128)S(1)}, f32[2304,192]{1,0:T(8,128)}, u32[]{:S(2)}) copy-start(f32[2304,192]{1,0:T(8,128)} %get-tuple-element.199) | copy-start | bytes 5308420 | tf_op jit(solution)/shard_map/while
  452.1 18.3 %copy-start.2 = (f32[2304,192]{1,0:T(8,128)S(1)}, f32[2304,192]{1,0:T(8,128)}, u32[]{:S(2)}) copy-start(f32[2304,192]{1,0:T(8,128)} %get-tuple-element.199) | copy-start | bytes 5308420 | tf_op jit(solution)/shard_map/while
  494.5 18.3 %copy-start.2 = (f32[2304,192]{1,0:T(8,128)S(1)}, f32[2304,192]{1,0:T(8,128)}, u32[]{:S(2)}) copy-start(f32[2304,192]{1,0:T(8,128)} %get-tuple-element.199) | copy-start | bytes 5308420 | tf_op jit(solution)/shard_map/while
  536.8 18.3 %copy-start.2 = (f32[2304,192]{1,0:T(8,128)S(1)}, f32[2304,192]{1,0:T(8,128)}, u32[]{:S(2)}) copy-start(f32[2304,192]{1,0:T(8,128)} %get-tuple-element.199) | copy-start | bytes 5308420 | tf_op jit(solution)/shard_map/while
  579.2 18.3 %copy-start.2 = (f32[2304,192]{1,0:T(8,128)S(1)}, f32[2304,192]{1,0:T(8,128)}, u32[]{:S(2)}) copy-start(f32[2304,192]{1,0:T(8,128)} %get-tuple-element.199) | copy-start | bytes 5308420 | tf_op jit(solution)/shard_map/while
  627.7 0.7 copy-start.5
  627.7 0.9 copy-start.3
  627.8 255.3 %all-reduce.5.cloned.1.call-start = ((), (), s32[]{:S(2)}) async-start(), calls=%async_computation.3 | async-start | bytes 393216 | tf_op jit(solution)/shard_map/psum | solution.py:90
  744.7 2.4 copy-start.1
Sparse Core Ops, SparseCore 0:
  12.7 79.7 all-gather.1
  627.9 116.7 all-reduce.2
  749.6 133.4 all-reduce.4
where the time goes:
time: 901 us; the launch traced here: 891 us
  waiting for transfers between devices  433 us (48%)
  matrix products  282 us (31%)
  local copies, waits for them, and re-layouts  127 us (14%)
  loops' own time  25.6 us (3%)
  between operations  13.4 us (1%)
    dot_general x8, matrix products, orbital_block(): jnp.dot(sine_part, right_sin, precision=lax.Precision.HIGHEST, preferred_...  146 us
    psum x1, waiting for transfers between devices, local(): return lax.psum(gradient, 'walk')  134 us
    dot_general x8, matrix products, orbital_block(): jnp.dot(cosine, right_cos, precision=lax.Precision.HIGHEST, preferred_ele...  131 us
    psum x1, waiting for transfers between devices, local(): orbitals = lax.psum(partial_value, 'band')  114 us
    all_to_all x1, waiting for transfers between devices, local(): lax.all_to_all(gathered, 'band', split_axis=1, concat_axis=2, tiled=True)  105 us
    all_gather x1, waiting for transfers between devices, local(): gathered = lax.all_gather(coefficients, 'walk', axis=1, tiled=True)  79.9 us
    dynamic_update_slice x16, local copies, waits for them, and re-layouts, local(): lax.map(lambda coords: orbital_block(coords[0], coords[1], lat_x, lat_y,...  60.7 us
    all_to_all x3, local copies, waits for them, and re-layouts, local(): lax.all_to_all(gathered, 'band', split_axis=1, concat_axis=2, tiled=True)  41.4 us
  transfers between devices with their start and end apart: 4, of which 4 were waited for; matrix products, arithmetic and copies ran while one was open for 0% of the time, Pallas kernels for 0%

commit v1 on v0

--- a/solution.py
+++ b/solution.py
@@ -85,7 +85,7 @@
     )
     partial_value = partial_value.reshape(local_count, right_cos.shape[1])
     walkers = float(walk_count * local_count // E)
-    orbitals = lax.psum(partial_value, "band")
+    orbitals = lax.all_gather(partial_value, "band").sum(axis=0)
     gradient = fit_gradient(orbitals, spin_labels, features, orbital_head, walkers)
     return lax.psum(gradient, "walk")
 

time: 901 us -> 1020 us (1.13)
  waiting for transfers between devices: 433 us -> 538 us
    all_gather x0 -> x1, waiting for transfers between devices: none -> 220 us  [local(): orbitals = lax.all_gather(partial_value, 'band').sum(axis=0)]
    psum x1 -> x0, waiting for transfers between devices: 114 us -> none  [local(): orbitals = lax.psum(partial_value, 'band')]
where the time goes in v1:
time: 1020 us; the launch traced here: 1010 us
  waiting for transfers between devices  538 us (53%)
  matrix products  282 us (28%)
  local copies, waits for them, and re-layouts  127 us (12%)
  loops' own time  26.9 us (3%)
  other arithmetic  15.6 us (2%)
  between operations  13.4 us (1%)
    all_gather x1, waiting for transfers between devices, local(): orbitals = lax.all_gather(partial_value, 'band').sum(axis=0)  220 us
    dot_general x8, matrix products, orbital_block(): jnp.dot(sine_part, right_sin, precision=lax.Precision.HIGHEST, preferred_...  146 us
    psum x1, waiting for transfers between devices, local(): return lax.psum(gradient, 'walk')  133 us
    dot_general x8, matrix products, orbital_block(): jnp.dot(cosine, right_cos, precision=lax.Precision.HIGHEST, preferred_ele...  131 us
    all_to_all x1, waiting for transfers between devices, local(): lax.all_to_all(gathered, 'band', split_axis=1, concat_axis=2, tiled=True)  105 us
    all_gather x1, waiting for transfers between devices, local(): gathered = lax.all_gather(coefficients, 'walk', axis=1, tiled=True)  79.9 us
    dynamic_update_slice x16, local copies, waits for them, and re-layouts, local(): lax.map(lambda coords: orbital_block(coords[0], coords[1], lat_x, lat_y,...  60.7 us
    all_to_all x3, local copies, waits for them, and re-layouts, local(): lax.all_to_all(gathered, 'band', split_axis=1, concat_axis=2, tiled=True)  41.4 us
  transfers between devices with their start and end apart: 4, of which 4 were waited for; matrix products, arithmetic and copies ran while one was open for 0% of the time, Pallas kernels for 0%

profile of v1, /device:TPU:0, one launch (start us, length us, event | category | flops | bytes accessed | tf_op | source)
XLA Modules:
  0.0 1008.0 jit_solution(3903076307778801097)
XLA Ops:
  6.5 6.1 copy.30
  12.7 79.9 %all-gather.3.cloned.1.call-done = bf16[2,18432,128]{2,0,1:T(2,128)(2,1)} async-done(((bf16[2,1152,128]{2,0,1:T(2,128)(2,1)}), bf16[2,18432,128]{2,0,1:T(2,128)(2,1)}) %all-gather.3.cloned.1.call-update) | async-done | bytes 9437200 | tf_op jit(solution)/shard_map/all_gather | solution.py:67
  92.5 5.0 all-to-all-start
  97.7 0.1 reshape.49
  97.7 0.1 reshape.48
  97.8 0.1 slice_reduce_fusion
  97.9 0.9 fusion.32
  98.9 105.0 %all-to-all-done = bf16[2,18432,128]{2,0,1:T(2,128)(2,1)} async-done(((bf16[2,18432,128]{2,0,1:T(2,128)(2,1)}), bf16[2,18432,128]{2,0,1:T(2,128)(2,1)}, u32[]{:S(2)}, u32[]{:S(2)}) %all-to-all-start) | async-done | bytes 9437216 | tf_op jit(solution)/shard_map/all_to_all | solution.py:68
  203.9 10.1 %copy.31 = bf16[2,18432,128]{2,1,0:T(8,128)(2,1)} copy(bf16[2,18432,128]{2,0,1:T(2,128)(2,1)} %all-to-all-done) | data formatting | bytes 18874368 | tf_op jit(solution)/shard_map/all_to_all | solution.py:68
  214.0 12.9 %copy.32 = bf16[2,2304,8,128]{1,3,2,0:T(8,128)(2,1)} copy(bf16[2,2304,8,128]{3,1,2,0:T(8,128)(2,1)} %bitcast.31) | data formatting | bytes 18874368 | tf_op jit(solution)/shard_map/all_to_all | solution.py:68
  226.9 18.4 %copy.33 = bf16[2,2304,1024]{1,0,2:T(2,128)(2,1)} copy(bf16[2,2304,1024]{1,2,0:T(8,128)(2,1)} %bitcast.32) | data formatting | bytes 18874368 | tf_op jit(solution)/shard_map/all_to_all | solution.py:68
  245.3 6.1 gather_fusion
  251.4 0.8 fusion.31
  252.2 1.2 fusion.37
  253.4 0.1 fusion.36
  253.5 0.1 copy.45
  253.6 1.5 maximum_convert_fusion.1
  255.0 3.0 copy.34
  258.0 1.9 copy.35
  259.9 365.6 %while.10 = (s32[]{:T(128)}, f32[8,384,192]{1,0,2:T(8,128)}, f32[8,384]{1,0:T(8,128)S(1)}, f32[2304]{0:T(1024)S(1)}, f32[8,384]{1,0:T(8,128)S(1)}, /*index=5*/f3...) while((s32[]{:T(128)}, f32[8,384,192]{1,0,2:T(8,128)}, ...), condition=%wide.region_1.2_spmd, body=%wide.region_0.1_spmd.sunk | while | flops 4084015104 | bytes 12730505 | solution.py:82
  282.6 18.3 %fusion.54 = f32[384,192]{0,1:T(8,128)S(1)} fusion(f32[2304,192]{1,0:T(8,128)} %get-tuple-element.200, f32[2304]{0:T(1024)S(1)} %get-tuple-element.198, f32[384]{0:T(512)S(1)} %get-tuple-element.171, f32[2304]{0:T(1024)S(1)} %get-tuple-element.196, f32[384]{0:T(512)S(1)} %get-tuple-element.172), kind=kOutput, calls=%fused_computation.1.clone.1 | convolution fusion | flops 2041970688 | bytes 2085888 | tf_op jit(solution)/shard_map/while/body/eval_jaxpr/dot_general | solution.py:17
  300.9 16.4 %fusion.55 = f32[1,384,192]{1,2,0:T(8,128)S(1)} fusion(f32[384,192]{0,1:T(8,128)S(1)} %fusion.54, f32[2304,192]{1,0:T(8,128)S(1)} %copy-done.2, f32[2304]{0:T(1024)S(1)} %get-tuple-element.198, f32[384]{0:T(512)S(1)} %get-tuple-element.171, f32[2304]{0:T(1024)S(1)} %get-tuple-element.196, f32[384]{0:T(512)S(1)} %get-tuple-element.172), kind=kOutput, calls=%fused_computation.17.clone.1 | convolution fusion | flops 2042044416 | bytes 2380800 | tf_op jit(solution)/shard_map/while/body/eval_jaxpr/dot_general | solution.py:14
  317.4 0.3 copy.47
  317.7 7.3 dynamic_update_slice.5
  325.0 18.3 %fusion.54 = f32[384,192]{0,1:T(8,128)S(1)} fusion(f32[2304,192]{1,0:T(8,128)} %get-tuple-element.200, f32[2304]{0:T(1024)S(1)} %get-tuple-element.198, f32[384]{0:T(512)S(1)} %get-tuple-element.171, f32[2304]{0:T(1024)S(1)} %get-tuple-element.196, f32[384]{0:T(512)S(1)} %get-tuple-element.172), kind=kOutput, calls=%fused_computation.1.clone.1 | convolution fusion | flops 2041970688 | bytes 2085888 | tf_op jit(solution)/shard_map/while/body/eval_jaxpr/dot_general | solution.py:17
  343.3 16.4 %fusion.55 = f32[1,384,192]{1,2,0:T(8,128)S(1)} fusion(f32[384,192]{0,1:T(8,128)S(1)} %fusion.54, f32[2304,192]{1,0:T(8,128)S(1)} %copy-done.2, f32[2304]{0:T(1024)S(1)} %get-tuple-element.198, f32[384]{0:T(512)S(1)} %get-tuple-element.171, f32[2304]{0:T(1024)S(1)} %get-tuple-element.196, f32[384]{0:T(512)S(1)} %get-tuple-element.172), kind=kOutput, calls=%fused_computation.17.clone.1 | convolution fusion | flops 2042044416 | bytes 2380800 | tf_op jit(solution)/shard_map/while/body/eval_jaxpr/dot_general | solution.py:14
  359.7 0.3 copy.47
  360.0 7.3 dynamic_update_slice.5
  367.4 18.3 %fusion.54 = f32[384,192]{0,1:T(8,128)S(1)} fusion(f32[2304,192]{1,0:T(8,128)} %get-tuple-element.200, f32[2304]{0:T(1024)S(1)} %get-tuple-element.198, f32[384]{0:T(512)S(1)} %get-tuple-element.171, f32[2304]{0:T(1024)S(1)} %get-tuple-element.196, f32[384]{0:T(512)S(1)} %get-tuple-element.172), kind=kOutput, calls=%fused_computation.1.clone.1 | convolution fusion | flops 2041970688 | bytes 2085888 | tf_op jit(solution)/shard_map/while/body/eval_jaxpr/dot_general | solution.py:17
  385.7 16.4 %fusion.55 = f32[1,384,192]{1,2,0:T(8,128)S(1)} fusion(f32[384,192]{0,1:T(8,128)S(1)} %fusion.54, f32[2304,192]{1,0:T(8,128)S(1)} %copy-done.2, f32[2304]{0:T(1024)S(1)} %get-tuple-element.198, f32[384]{0:T(512)S(1)} %get-tuple-element.171, f32[2304]{0:T(1024)S(1)} %get-tuple-element.196, f32[384]{0:T(512)S(1)} %get-tuple-element.172), kind=kOutput, calls=%fused_computation.17.clone.1 | convolution fusion | flops 2042044416 | bytes 2380800 | tf_op jit(solution)/shard_map/while/body/eval_jaxpr/dot_general | solution.py:14
  402.1 0.3 copy.47
  402.4 7.3 dynamic_update_slice.5
  409.7 18.3 %fusion.54 = f32[384,192]{0,1:T(8,128)S(1)} fusion(f32[2304,192]{1,0:T(8,128)} %get-tuple-element.200, f32[2304]{0:T(1024)S(1)} %get-tuple-element.198, f32[384]{0:T(512)S(1)} %get-tuple-element.171, f32[2304]{0:T(1024)S(1)} %get-tuple-element.196, f32[384]{0:T(512)S(1)} %get-tuple-element.172), kind=kOutput, calls=%fused_computation.1.clone.1 | convolution fusion | flops 2041970688 | bytes 2085888 | tf_op jit(solution)/shard_map/while/body/eval_jaxpr/dot_general | solution.py:17
  428.1 16.4 %fusion.55 = f32[1,384,192]{1,2,0:T(8,128)S(1)} fusion(f32[384,192]{0,1:T(8,128)S(1)} %fusion.54, f32[2304,192]{1,0:T(8,128)S(1)} %copy-done.2, f32[2304]{0:T(1024)S(1)} %get-tuple-element.198, f32[384]{0:T(512)S(1)} %get-tuple-element.171, f32[2304]{0:T(1024)S(1)} %get-tuple-element.196, f32[384]{0:T(512)S(1)} %get-tuple-element.172), kind=kOutput, calls=%fused_computation.17.clone.1 | convolution fusion | flops 2042044416 | bytes 2380800 | tf_op jit(solution)/shard_map/while/body/eval_jaxpr/dot_general | solution.py:14
  444.5 0.3 copy.47
  444.8 7.3 dynamic_update_slice.5
  452.1 18.3 %fusion.54 = f32[384,192]{0,1:T(8,128)S(1)} fusion(f32[2304,192]{1,0:T(8,128)} %get-tuple-element.200, f32[2304]{0:T(1024)S(1)} %get-tuple-element.198, f32[384]{0:T(512)S(1)} %get-tuple-element.171, f32[2304]{0:T(1024)S(1)} %get-tuple-element.196, f32[384]{0:T(512)S(1)} %get-tuple-element.172), kind=kOutput, calls=%fused_computation.1.clone.1 | convolution fusion | flops 2041970688 | bytes 2085888 | tf_op jit(solution)/shard_map/while/body/eval_jaxpr/dot_general | solution.py:17
  470.4 16.4 %fusion.55 = f32[1,384,192]{1,2,0:T(8,128)S(1)} fusion(f32[384,192]{0,1:T(8,128)S(1)} %fusion.54, f32[2304,192]{1,0:T(8,128)S(1)} %copy-done.2, f32[2304]{0:T(1024)S(1)} %get-tuple-element.198, f32[384]{0:T(512)S(1)} %get-tuple-element.171, f32[2304]{0:T(1024)S(1)} %get-tuple-element.196, f32[384]{0:T(512)S(1)} %get-tuple-element.172), kind=kOutput, calls=%fused_computation.17.clone.1 | convolution fusion | flops 2042044416 | bytes 2380800 | tf_op jit(solution)/shard_map/while/body/eval_jaxpr/dot_general | solution.py:14
  486.9 0.3 copy.47
  487.2 7.3 dynamic_update_slice.5
  494.5 18.3 %fusion.54 = f32[384,192]{0,1:T(8,128)S(1)} fusion(f32[2304,192]{1,0:T(8,128)} %get-tuple-element.200, f32[2304]{0:T(1024)S(1)} %get-tuple-element.198, f32[384]{0:T(512)S(1)} %get-tuple-element.171, f32[2304]{0:T(1024)S(1)} %get-tuple-element.196, f32[384]{0:T(512)S(1)} %get-tuple-element.172), kind=kOutput, calls=%fused_computation.1.clone.1 | convolution fusion | flops 2041970688 | bytes 2085888 | tf_op jit(solution)/shard_map/while/body/eval_jaxpr/dot_general | solution.py:17
  512.8 16.4 %fusion.55 = f32[1,384,192]{1,2,0:T(8,128)S(1)} fusion(f32[384,192]{0,1:T(8,128)S(1)} %fusion.54, f32[2304,192]{1,0:T(8,128)S(1)} %copy-done.2, f32[2304]{0:T(1024)S(1)} %get-tuple-element.198, f32[384]{0:T(512)S(1)} %get-tuple-element.171, f32[2304]{0:T(1024)S(1)} %get-tuple-element.196, f32[384]{0:T(512)S(1)} %get-tuple-element.172), kind=kOutput, calls=%fused_computation.17.clone.1 | convolution fusion | flops 2042044416 | bytes 2380800 | tf_op jit(solution)/shard_map/while/body/eval_jaxpr/dot_general | solution.py:14
  529.2 0.3 copy.47
  529.5 7.3 dynamic_update_slice.5
  536.9 18.3 %fusion.54 = f32[384,192]{0,1:T(8,128)S(1)} fusion(f32[2304,192]{1,0:T(8,128)} %get-tuple-element.200, f32[2304]{0:T(1024)S(1)} %get-tuple-element.198, f32[384]{0:T(512)S(1)} %get-tuple-element.171, f32[2304]{0:T(1024)S(1)} %get-tuple-element.196, f32[384]{0:T(512)S(1)} %get-tuple-element.172), kind=kOutput, calls=%fused_computation.1.clone.1 | convolution fusion | flops 2041970688 | bytes 2085888 | tf_op jit(solution)/shard_map/while/body/eval_jaxpr/dot_general | solution.py:17
  555.2 16.4 %fusion.55 = f32[1,384,192]{1,2,0:T(8,128)S(1)} fusion(f32[384,192]{0,1:T(8,128)S(1)} %fusion.54, f32[2304,192]{1,0:T(8,128)S(1)} %copy-done.2, f32[2304]{0:T(1024)S(1)} %get-tuple-element.198, f32[384]{0:T(512)S(1)} %get-tuple-element.171, f32[2304]{0:T(1024)S(1)} %get-tuple-element.196, f32[384]{0:T(512)S(1)} %get-tuple-element.172), kind=kOutput, calls=%fused_computation.17.clone.1 | convolution fusion | flops 2042044416 | bytes 2380800 | tf_op jit(solution)/shard_map/while/body/eval_jaxpr/dot_general | solution.py:14
  571.6 0.3 copy.47
  571.9 7.3 dynamic_update_slice.5
  579.2 18.3 %fusion.54 = f32[384,192]{0,1:T(8,128)S(1)} fusion(f32[2304,192]{1,0:T(8,128)} %get-tuple-element.200, f32[2304]{0:T(1024)S(1)} %get-tuple-element.198, f32[384]{0:T(512)S(1)} %get-tuple-element.171, f32[2304]{0:T(1024)S(1)} %get-tuple-element.196, f32[384]{0:T(512)S(1)} %get-tuple-element.172), kind=kOutput, calls=%fused_computation.1.clone.1 | convolution fusion | flops 2041970688 | bytes 2085888 | tf_op jit(solution)/shard_map/while/body/eval_jaxpr/dot_general | solution.py:17
  597.6 16.4 %fusion.55 = f32[1,384,192]{1,2,0:T(8,128)S(1)} fusion(f32[384,192]{0,1:T(8,128)S(1)} %fusion.54, f32[2304,192]{1,0:T(8,128)S(1)} %copy-done.2, f32[2304]{0:T(1024)S(1)} %get-tuple-element.198, f32[384]{0:T(512)S(1)} %get-tuple-element.171, f32[2304]{0:T(1024)S(1)} %get-tuple-element.196, f32[384]{0:T(512)S(1)} %get-tuple-element.172), kind=kOutput, calls=%fused_computation.17.clone.1 | convolution fusion | flops 2042044416 | bytes 2380800 | tf_op jit(solution)/shard_map/while/body/eval_jaxpr/dot_general | solution.py:14
  614.0 0.3 copy.47
  614.3 7.3 dynamic_update_slice.5
  625.6 3.2 all_gather_reshape.3
  628.9 0.6 copy-done.5
  629.5 0.2 copy-done.3
  629.7 2.1 fusion.38
  631.8 220.4 %all-gather.5.cloned.1.call-done = f32[8,3072,192]{1,2,0:T(8,128)} async-done(((f32[1,3072,192]{1,2,0:T(8,128)}), f32[8,3072,192]{1,2,0:T(8,128)}) %all-gather.5.cloned.1.call-update) | async-done | bytes 18874384 | tf_op jit(solution)/shard_map/all_gather | solution.py:88
  852.2 10.0 reduce_sum.9
  862.2 1.9 slice_select_fusion.2
  864.0 0.5 copy-done.1
  864.5 0.4 broadcast_select_fusion.2
  864.9 1.9 fusion.28
  866.9 132.7 %all-reduce.2.cloned.1.call-done = f32[256,192]{0,1:T(8,128)} async-done(((f32[256,192]{0,1:T(8,128)}), f32[256,192]{0,1:T(8,128)}) %all-reduce.2.cloned.1.call-update) | async-done | bytes 196624 | tf_op jit(solution)/shard_map/psum | solution.py:90
  999.6 1.6 copy.56
  (46 shorter events, 0.4 us)
Async XLA Ops:
  6.5 623.0 %copy-start = (bf16[3072,256]{1,0:T(8,128)(2,1)S(1)}, bf16[3072,256]{1,0:T(8,128)(2,1)}, u32[]{:S(2)}) copy-start(bf16[3072,256]{1,0:T(8,128)(2,1)} %param.14) | copy-start | bytes 4718596
  6.5 86.0 %all-gather.3.cloned.1.call-start = ((), (), s32[]{:S(2)}) async-start(), calls=%async_computation.1 | async-start | bytes 10027008 | tf_op jit(solution)/shard_map/all_gather | solution.py:67
  12.6 85.0 %copy-start.6 = (s32[2,48]{1,0:T(2,128)S(1)}, s32[2,48]{1,0:T(2,128)}, u32[]{:S(2)}) copy-start(s32[2,48]{1,0:T(2,128)} %param.13) | copy-start | bytes 1156
  12.6 85.2 %copy-start.4 = (f32[2,3072]{1,0:T(2,128)S(1)}, f32[2,3072]{1,0:T(2,128)}, u32[]{:S(2)}) copy-start(f32[2,3072]{1,0:T(2,128)} %param.9) | copy-start | bytes 73732
  92.5 111.3 %all-to-all-start = ((bf16[2,18432,128]{2,0,1:T(2,128)(2,1)}), bf16[2,18432,128]{2,0,1:T(2,128)(2,1)}, u32[]{:S(2)}, u32[]{:S(2)}) async-start(bf16[2,18432,128]{2,0,1:T(2,128)(2,1)} %all-gather.3.cloned.1.call-done), calls=%async_computation | async-start | bytes 18874368 | tf_op jit(solution)/shard_map/all_to_all | solution.py:68
  97.6 754.6 %all-gather.5.cloned.1.call-start = ((), (), s32[]{:S(2)}) async-start(), calls=%async_computation.2 | async-start | bytes 21233664 | tf_op jit(solution)/shard_map/all_gather | solution.py:88
  282.6 18.3 %copy-start.2 = (f32[2304,192]{1,0:T(8,128)S(1)}, f32[2304,192]{1,0:T(8,128)}, u32[]{:S(2)}) copy-start(f32[2304,192]{1,0:T(8,128)} %get-tuple-element.199) | copy-start | bytes 5308420 | tf_op jit(solution)/shard_map/while
  325.0 18.3 %copy-start.2 = (f32[2304,192]{1,0:T(8,128)S(1)}, f32[2304,192]{1,0:T(8,128)}, u32[]{:S(2)}) copy-start(f32[2304,192]{1,0:T(8,128)} %get-tuple-element.199) | copy-start | bytes 5308420 | tf_op jit(solution)/shard_map/while
  367.3 18.3 %copy-start.2 = (f32[2304,192]{1,0:T(8,128)S(1)}, f32[2304,192]{1,0:T(8,128)}, u32[]{:S(2)}) copy-start(f32[2304,192]{1,0:T(8,128)} %get-tuple-element.199) | copy-start | bytes 5308420 | tf_op jit(solution)/shard_map/while
  409.7 18.3 %copy-start.2 = (f32[2304,192]{1,0:T(8,128)S(1)}, f32[2304,192]{1,0:T(8,128)}, u32[]{:S(2)}) copy-start(f32[2304,192]{1,0:T(8,128)} %get-tuple-element.199) | copy-start | bytes 5308420 | tf_op jit(solution)/shard_map/while
  452.1 18.3 %copy-start.2 = (f32[2304,192]{1,0:T(8,128)S(1)}, f32[2304,192]{1,0:T(8,128)}, u32[]{:S(2)}) copy-start(f32[2304,192]{1,0:T(8,128)} %get-tuple-element.199) | copy-start | bytes 5308420 | tf_op jit(solution)/shard_map/while
  494.5 18.3 %copy-start.2 = (f32[2304,192]{1,0:T(8,128)S(1)}, f32[2304,192]{1,0:T(8,128)}, u32[]{:S(2)}) copy-start(f32[2304,192]{1,0:T(8,128)} %get-tuple-element.199) | copy-start | bytes 5308420 | tf_op jit(solution)/shard_map/while
  536.8 18.3 %copy-start.2 = (f32[2304,192]{1,0:T(8,128)S(1)}, f32[2304,192]{1,0:T(8,128)}, u32[]{:S(2)}) copy-start(f32[2304,192]{1,0:T(8,128)} %get-tuple-element.199) | copy-start | bytes 5308420 | tf_op jit(solution)/shard_map/while
  579.2 18.3 %copy-start.2 = (f32[2304,192]{1,0:T(8,128)S(1)}, f32[2304,192]{1,0:T(8,128)}, u32[]{:S(2)}) copy-start(f32[2304,192]{1,0:T(8,128)} %get-tuple-element.199) | copy-start | bytes 5308420 | tf_op jit(solution)/shard_map/while
  628.8 0.7 copy-start.5
  628.8 0.9 copy-start.3
  628.8 370.8 %all-reduce.2.cloned.1.call-start = ((), (), s32[]{:S(2)}) async-start(), calls=%async_computation.3 | async-start | bytes 393216 | tf_op jit(solution)/shard_map/psum | solution.py:90
  862.2 2.4 copy-start.1
Sparse Core Ops, SparseCore 0:
  12.7 79.7 all-gather.2
  628.9 223.1 all-gather.4
  867.0 132.5 all-reduce.1
